TPU v7x, 32 devices: a whole 2x2x4 slice. The times are simulated.
32 devices in a mesh: grp: 4 (over x, core), tp: 4 (over z), cores: 2 (over y).
Axes of the slice: x: 2, y: 2, z: 4, core: 2. Of those that a mesh axis runs over, the one named last changes fastest.
Arguments:
- tokens: bfloat16 [4096, 8192], P('grp', ('tp', 'cores')), may hold values from -6 to 6
- gate_up_weight: bfloat16 [8192, 2, 16384], P(None, None, ('tp', 'cores')), may hold values from -0.0625 to 0.0625
- down_factor_pool: bfloat16 [8, 8192, 256], P(('tp', 'cores'), 'grp'), may hold values from -0.0625 to 0.0625
- up_factor_pool: bfloat16 [8, 4, 8, 128, 1024], P(('tp', 'cores'), 'grp'), may hold values from -0.5 to 0.5
- segment_adapters: int32 [4, 3], replicated, may hold values from 0 to 7
- segment_tile_counts: int32 [4, 3], P('grp'), may hold values from 1 to 4, 8 in all within a row
- adapter_pool_rows: int32 [8], replicated, may hold values from 0 to 7, each once
Outputs:
- hidden: bfloat16 [4096, 16384], P('grp', ('tp', 'cores'))
Inputs may be any that keep to these rules, and one draw needn't show every extreme that they name: `segment_tile_counts`: each row sums to 8. `adapter_pool_rows`: each pool row appears once.
All inputs are finite; a program needn't handle non-finite values.
Results may differ from a plain program's by a relative error of at most 0.0036.
Values may be sent and summed in bfloat16 or wider, within the bound.
A program may use at most 320 MiB of HBM per device.

v0:
```python
import jax
import jax.numpy as jnp
from jax import lax
from jax.sharding import PartitionSpec as P

TILE = 128
adapter_scale = 0.5


def tile_segments(tile_lengths, tile_count):
    bounds = jnp.cumsum(tile_lengths)
    positions = jnp.arange(tile_count, dtype=jnp.int32)
    return jnp.sum((bounds[None, :] <= positions[:, None]).astype(jnp.int32), axis=1)


def per_device(
    tokens,
    gate_up_weight,
    down_factor_pool,
    up_factor_pool,
    segment_adapters,
    segment_tile_counts,
    adapter_pool_rows,
):
    groups = lax.axis_size("grp")
    device_shares = lax.axis_size(("tp", "cores"))
    piece_index = lax.axis_index(("tp", "cores"))
    token_count = tokens.shape[0]
    full_width = tokens.shape[1] * device_shares
    local_hidden_width = gate_up_weight.shape[2]
    twice_rank = down_factor_pool.shape[2]
    rank_size = twice_rank // 2
    share_rows = down_factor_pool.shape[1] // device_shares
    local_count = down_factor_pool.shape[0]
    seg_count = segment_adapters.shape[1]
    narrow = local_hidden_width // groups
    local_down_factor = down_factor_pool.reshape(
        local_count, device_shares, share_rows * twice_rank
    )
    local_up_factor = up_factor_pool.reshape(local_count, device_shares, -1)
    a_spread, b_spread = (
        lax.all_to_all(local_down_factor, ("tp", "cores"), split_axis=1, concat_axis=0, tiled=True),
        lax.all_to_all(local_up_factor, ("tp", "cores"), split_axis=1, concat_axis=0, tiled=True),
    )
    all_slots = jnp.take(adapter_pool_rows, segment_adapters)
    a_wanted = jnp.take(a_spread, all_slots, axis=0)
    b_wanted = jnp.take(b_spread, all_slots, axis=0)
    a_arrived, b_arrived = (
        lax.all_to_all(a_wanted, "grp", split_axis=0, concat_axis=2, tiled=True),
        lax.all_to_all(b_wanted, "grp", split_axis=0, concat_axis=2, tiled=True),
    )
    a_chosen = a_arrived.reshape(seg_count, groups, -1)
    b_chosen = b_arrived.reshape(seg_count, groups, -1)
    gathered = lax.all_gather(tokens, ("tp", "cores"), axis=1, tiled=True)
    frozen_output = jnp.dot(
        gathered,
        gate_up_weight.reshape(full_width, 2 * local_hidden_width),
        preferred_element_type=jnp.float32,
    )
    frozen_output = frozen_output.reshape(token_count, 2, local_hidden_width)
    tile_count = token_count // TILE
    tile_seg = tile_segments(segment_tile_counts[0], tile_count)
    a_tiles = jnp.take(a_chosen, tile_seg, axis=0).reshape(
        tile_count, groups * share_rows, twice_rank
    )
    own_features = lax.dynamic_slice_in_dim(
        gathered.reshape(token_count, groups, device_shares, share_rows), piece_index, 1, axis=2
    )
    own_features = own_features.reshape(tile_count, TILE, groups * share_rows)
    partial_shrink = jnp.einsum(
        "tkd,tdr->tkr", own_features, a_tiles, preferred_element_type=jnp.float32
    )
    reduced_input = lax.psum(partial_shrink, ("tp", "cores")).astype(jnp.bfloat16)
    b_tiles = jnp.take(b_chosen, tile_seg, axis=0).reshape(tile_count, groups, rank_size, 2, narrow)
    gate_adapter_delta = jnp.einsum(
        "tkr,tmrw->tkmw",
        reduced_input[:, :, :rank_size],
        b_tiles[:, :, :, 0, :],
        preferred_element_type=jnp.float32,
    )
    up_adapter_delta = jnp.einsum(
        "tkr,tmrw->tkmw",
        reduced_input[:, :, rank_size:],
        b_tiles[:, :, :, 1, :],
        preferred_element_type=jnp.float32,
    )
    gate_combined = frozen_output[:, 0, :] + adapter_scale * gate_adapter_delta.reshape(
        token_count, local_hidden_width
    )
    up_combined = frozen_output[:, 1, :] + adapter_scale * up_adapter_delta.reshape(
        token_count, local_hidden_width
    )
    return (jax.nn.silu(gate_combined) * up_combined).astype(jnp.bfloat16)


def solution(mesh):
    return jax.shard_map(
        per_device,
        mesh=mesh,
        in_specs=(
            P("grp", ("tp", "cores")),
            P(None, None, ("tp", "cores")),
            P(("tp", "cores"), "grp", None),
            P(("tp", "cores"), "grp", None, None, None),
            P(),
            P("grp", None),
            P(),
        ),
        out_specs=P("grp", ("tp", "cores")),
        check_vma=False,
    )
```

profile of v0, /device:TPU:0, one launch (start us, length us, event | category | flops | bytes accessed | tf_op | source)
XLA Modules:
  0.0 634.1 jit_solution(12954752661760870075)
XLA Ops:
  11.1 7.3 %reduce.3 = bf16[8,65536]{1,0:T(8,128)(2,1)S(1)} reduce(bf16[8,1,65536]{2,1,0:T(2,128)(2,1)S(1)} %bitcast.106, bf16[]{:T(256)} %broadcast.154), dimensions={1}, to_apply=%bitcast.85.reduce_sub_computation | reduce | bytes 2097154
  20.3 7.5 %all-to-all-start = ((bf16[8,2,32768]{2,1,0:T(2,128)(2,1)}), bf16[8,2,32768]{2,1,0:T(2,128)(2,1)S(1)}, u32[]{:S(2)}, u32[]{:S(2)}) async-start(bf16[8,2,32768]{2,1,0:T(2,128)(2,1)} %reshape.206), calls=%async_computation | async-start | bytes 2097152 | tf_op jit(solution)/shard_map/all_to_all | solution.py:42
  32.9 13.0 %reduce.2 = bf16[8,131072]{1,0:T(8,128)(2,1)S(1)} reduce(bf16[8,1,131072]{2,1,0:T(2,128)(2,1)} %bitcast.100, bf16[]{:T(256)} %broadcast.154), dimensions={1}, to_apply=%bitcast.83.reduce_sub_computation | reduce | bytes 4194306
  49.1 4.4 all-to-all-done
  58.1 5.8 reshape.207
  77.6 28.9 %all-to-all-done.2 = bf16[8,2,65536]{2,1,0:T(2,128)(2,1)S(1)} async-done(((bf16[8,2,65536]{2,1,0:T(2,128)(2,1)}), bf16[8,2,65536]{2,1,0:T(2,128)(2,1)S(1)}, u32[]{:S(2)}, u32[]{:S(2)}) %all-to-all-start.2) | async-done | bytes 2097184 | tf_op jit(solution)/shard_map/all_to_all | solution.py:43
  106.5 4.7 all-to-all-start.1
  115.5 4.5 copy.79
  131.6 5.8 fusion.8
  137.3 5.0 all-to-all-start.3
  143.2 45.1 %copy.69 = bf16[1024,8,2,2048]{3,1,2,0:T(8,128)(2,1)} copy(bf16[1024,8,2,2048]{3,2,1,0:T(2,128)(2,1)} %bitcast.33) | data formatting | bytes 134217728
  188.3 83.4 %copy.48 = bf16[4096,8192]{1,0:T(8,128)(2,1)} copy(bf16[4096,8192]{0,1:T(8,128)(2,1)} %bitcast.1) | data formatting | bytes 134217728 | tf_op jit(solution)/shard_map/dot_general | solution.py:55
  274.9 5.4 gather_fusion.2
  280.3 7.9 %gather.27 = bf16[8,1024,256]{2,1,0:T(8,128)(2,1)} reshape(bf16[8,4,65536]{2,1,0:T(4,128)(2,1)} %gather_fusion.2) | data formatting | bytes 8388608 | tf_op jit(solution)/shard_map/jit(_take)/gather | solution.py:63
  288.3 5.2 copy.78
  294.5 5.4 gather_fusion.5
  299.9 5.5 gather_fusion.6
  305.4 8.3 %pad_maximum_fusion = bf16[8,4,131072]{2,1,0:T(4,128)(2,1)} fusion(bf16[8,4,65536]{2,1,0:T(4,128)(2,1)} %gather_fusion.6, bf16[8,4,65536]{2,1,0:T(4,128)(2,1)} %gather_fusion.5), kind=kLoop, calls=%fused_computation.15 | loop fusion | flops 16777216 | bytes 16777216
  313.8 12.5 %reshape.201 = bf16[8,4,128,2,512]{4,3,2,1,0:T(2,128)(2,1)} reshape(bf16[8,4,131072]{2,1,0:T(4,128)(2,1)} %pad_maximum_fusion) | data formatting | bytes 16777216 | tf_op jit(solution)/shard_map/jit(_take)/gather | solution.py:74
  326.3 8.2 %copy_select_fusion = bf16[8,4,128,2,512]{4,2,1,0,3:T(8,128)(2,1)} fusion(bf16[8,4,128,2,512]{4,3,2,1,0:T(2,128)(2,1)} %reshape.201, pred[8]{0:T(512)(128)(4,1)S(1)} %compare_and_fusion.1), kind=kLoop, calls=%fused_computation.16 | loop fusion | flops 4194304 | bytes 16777224 | tf_op jit(solution)/shard_map/jit(_take)/select_n | solution.py:74
  334.6 37.6 %all-gather.2.cloned.1.call-done = bf16[1024,8192]{1,0:T(8,128)(2,1)} async-done(((bf16[1024,1024]{1,0:T(8,128)(2,1)}), bf16[1024,8192]{1,0:T(8,128)(2,1)}) %all-gather.2.cloned.1.call-update) | async-done | bytes 16777232 | tf_op jit(solution)/shard_map/all_gather | solution.py:54
  372.2 10.3 %copy.70 = bf16[128,8,32,256]{3,2,1,0:T(8,128)(2,1)S(1)} copy(bf16[128,8,32,256]{3,1,2,0:T(8,128)(2,1)} %bitcast.102) | data formatting | bytes 33554432
  382.4 13.7 %dynamic-slice_reduce_fusion = bf16[1024,4,256]{2,1,0:T(4,128)(2,1)S(1)} fusion(bf16[1024,4,8,256]{3,2,1,0:T(8,128)(2,1)S(1)} %bitcast.98, s32[]{:T(128)S(6)} %select_n.80), kind=kLoop, calls=%fused_computation.27 | loop fusion | bytes 4194308 | tf_op jit(solution)/shard_map/dynamic_slice | solution.py:66
  402.6 70.0 %all-reduce.1 = bf16[8,128,256]{2,1,0:T(8,128)(2,1)S(1)} all-reduce(f32[8,128,256]{2,1,0:T(8,128)S(1)} %fusion.9), channel_id=1, replica_groups=mesh['grp'=4,'tp'=4,'cores'=2] {'tp','cores'}, use_global_device_ids=true, to_apply=%region_2.3 | all-reduce | flops 262144 | bytes 1572864 | tf_op jit(solution)/shard_map/psum | solution.py:73
  472.6 6.6 %broadcast_multiply_fusion.1 = f32[8,128,4,512]{3,1,2,0:T(8,128)} fusion(bf16[8,4,128,2,512]{4,2,1,0,3:T(8,128)(2,1)} %copy_select_fusion, bf16[8,128,256]{2,1,0:T(8,128)(2,1)S(1)} %all-reduce.1), kind=kOutput, calls=%fused_computation.24 | convolution fusion | flops 538968064 | bytes 12845056 | tf_op jit(solution)/shard_map/tkr,tmrw->tkmw/dot_general | solution.py:75
  479.2 6.6 %broadcast_multiply_fusion = f32[8,128,4,512]{3,1,2,0:T(8,128)} fusion(bf16[8,4,128,2,512]{4,2,1,0,3:T(8,128)(2,1)} %copy_select_fusion, bf16[8,128,256]{2,1,0:T(8,128)(2,1)S(1)} %all-reduce.1), kind=kOutput, calls=%fused_computation.23 | convolution fusion | flops 538968064 | bytes 12845056 | tf_op jit(solution)/shard_map/tkr,tmrw->tkmw/dot_general | solution.py:81
  485.8 12.1 %copy.60 = f32[8,128,4,512]{3,2,1,0:T(4,128)} copy(f32[8,128,4,512]{3,1,2,0:T(8,128)} %broadcast_multiply_fusion) | data formatting | bytes 16777216 | tf_op jit(solution)/shard_map/mul | solution.py:90
  497.9 11.1 %copy.72 = f32[128,8,4,512]{3,1,2,0:T(8,128)} copy(f32[128,8,4,512]{3,2,1,0:T(4,128)} %bitcast.94) | data formatting | bytes 16777216
  509.0 12.1 %copy.59 = f32[8,128,4,512]{3,2,1,0:T(4,128)} copy(f32[8,128,4,512]{3,1,2,0:T(8,128)} %broadcast_multiply_fusion.1) | data formatting | bytes 16777216 | tf_op jit(solution)/shard_map/mul | solution.py:87
  521.0 10.8 %copy.71 = f32[128,8,4,512]{3,1,2,0:T(8,128)} copy(f32[128,8,4,512]{3,2,1,0:T(4,128)} %bitcast.95) | data formatting | bytes 16777216
  531.8 80.5 %fusion = f32[1024,2,2048]{2,0,1:T(8,128)} fusion(bf16[2,2048,8192]{2,1,0:T(8,128)(2,1)} %bitcast.2, bf16[1024,8192]{1,0:T(8,128)(2,1)} %all-gather.2.cloned.1.call-done), kind=kOutput, calls=%fused_computation.7 | convolution fusion | flops 68719476736 | bytes 100663296 | tf_op jit(solution)/shard_map/dot_general | solution.py:55
  612.3 14.8 %fusion.4 = bf16[1024,2048]{1,0:T(8,128)(2,1)} fusion(f32[1024,2048]{1,0:T(8,128)} %bitcast.96, f32[1024,2,2048]{2,0,1:T(8,128)} %fusion, f32[1024,2048]{1,0:T(8,128)} %bitcast.97), kind=kLoop, calls=%fused_computation.12 | loop fusion | flops 16777216 | bytes 37748736 | tf_op jit(solution)/shard_map/convert_element_type | solution.py:93
  (49 shorter events, 60.6 us)
Async XLA Ops:
  6.5 21.4 %copy-start = (s32[8]{0:T(128)S(1)}, s32[8]{0:T(128)}, u32[]{:S(2)}) copy-start(s32[8]{0:T(128)} %param.13) | copy-start | bytes 100
  10.5 17.3 %copy-start.4 = (s32[4,3]{1,0:T(4,128)S(1)}, s32[4,3]{1,0:T(4,128)}, u32[]{:S(2)}) copy-start(s32[4,3]{1,0:T(4,128)} %param.11) | copy-start | bytes 148
  18.4 10.4 %copy-start.3 = (bf16[1,1,8,128,1024]{4,3,2,1,0:T(8,128)(2,1)S(1)}, bf16[1,1,8,128,1024]{4,3,2,1,0:T(8,128)(2,1)}, u32[]{:S(2)}) copy-start(bf16[1,1,8,128,1024]{4,3,2,1,0:T(8,128)(2,1)} %param.10) | copy-start | bytes 6291460
  20.3 33.2 %all-to-all-start = ((bf16[8,2,32768]{2,1,0:T(2,128)(2,1)}), bf16[8,2,32768]{2,1,0:T(2,128)(2,1)S(1)}, u32[]{:S(2)}, u32[]{:S(2)}) async-start(bf16[8,2,32768]{2,1,0:T(2,128)(2,1)} %reshape.206), calls=%async_computation | async-start | bytes 2097152 | tf_op jit(solution)/shard_map/all_to_all | solution.py:42
  53.5 1.0 copy-start.2
  54.5 52.0 %all-to-all-start.2 = ((bf16[8,2,65536]{2,1,0:T(2,128)(2,1)}), bf16[8,2,65536]{2,1,0:T(2,128)(2,1)S(1)}, u32[]{:S(2)}, u32[]{:S(2)}) async-start(bf16[8,2,65536]{2,1,0:T(2,128)(2,1)} %reshape.204), calls=%async_computation.2 | async-start | bytes 4194304 | tf_op jit(solution)/shard_map/all_to_all | solution.py:43
  106.5 30.8 %all-to-all-start.1 = ((bf16[4,3,1,65536]{3,1,2,0:T(4,128)(2,1)}), bf16[4,3,1,65536]{3,1,2,0:T(4,128)(2,1)}, u32[]{:S(2)}, u32[]{:S(2)}) async-start(bf16[4,3,1,65536]{3,1,2,0:T(4,128)(2,1)} %select_bitcast_fusion), calls=%async_computation.1 | async-start | bytes 4194304 | tf_op jit(solution)/shard_map/all_to_all | solution.py:49
  137.3 5.7 copy-start.5
  137.3 150.9 %all-to-all-start.3 = ((bf16[4,3,1,131072]{3,1,2,0:T(4,128)(2,1)}), bf16[4,3,1,131072]{3,1,2,0:T(4,128)(2,1)}, u32[]{:S(2)}, u32[]{:S(2)}) async-start(bf16[4,3,1,131072]{3,1,2,0:T(4,128)(2,1)} %fusion.8), calls=%async_computation.3 | async-start | bytes 8388608 | tf_op jit(solution)/shard_map/all_to_all | solution.py:50
  142.3 229.8 %all-gather.2.cloned.1.call-start = ((), (), s32[]{:S(2)}) async-start(), calls=%async_computation.4 | async-start | bytes 18874368 | tf_op jit(solution)/shard_map/all_gather | solution.py:54
  612.3 14.8 %copy-start.1 = (s32[8]{0:T(128)S(1)}, s32[8]{0:T(128)}, u32[]{:S(2)}) copy-start(s32[8]{0:T(128)} %param.13) | copy-start | bytes 100
Sparse Core Ops, SparseCore 0:
  145.3 226.8 all-gather.1
where the time goes:
time: 644 us; the launch traced here: 634 us
  local copies, waits for them, and re-layouts  299 us (46%)
  matrix products  97.5 us (15%)
  waiting for transfers between devices  71.2 us (11%)
  blocking collectives  70 us (11%)
  other arithmetic  61.6 us (10%)
  starting transfers between devices  21.2 us (3%)
  between operations  13.8 us (2%)
    unnamed x23, local copies, waits for them, and re-layouts  101 us
    dot_general x1, local copies, waits for them, and re-layouts, per_device(): jnp.dot(gathered, gate_up_weight.reshape(full_width, 2 * local_hidden_wid...  83.4 us
    dot_general x1, matrix products, per_device(): jnp.dot(gathered, gate_up_weight.reshape(full_width, 2 * local_hidden_wid...  80.5 us
    psum x1, blocking collectives, per_device(): lax.psum(partial_shrink, ('tp', 'cores')).astype(jnp.bfloat16)  70 us
    all_gather x1, waiting for transfers between devices, per_device(): gathered = lax.all_gather(tokens, ('tp', 'cores'), axis=1, tiled=True)  37.6 us
    all_to_all x1, waiting for transfers between devices, per_device(): lax.all_to_all(local_up_factor, ('tp', 'cores'), split_axis=1, concat_axi...  28.9 us
    unnamed x3, other arithmetic  28.6 us
    gather x4, local copies, waits for them, and re-layouts, per_device(): jnp.take(b_chosen, tile_seg, axis=0)  24.6 us
  transfers between devices with their start and end apart: 5, of which 3 were waited for; matrix products, arithmetic and copies ran while one was open for 41% of the time, Pallas kernels for 0%

commit v1 on v0

--- a/solution.py
+++ b/solution.py
@@ -70,7 +70,9 @@
     partial_shrink = jnp.einsum(
         "tkd,tdr->tkr", own_features, a_tiles, preferred_element_type=jnp.float32
     )
-    reduced_input = lax.psum(partial_shrink, ("tp", "cores")).astype(jnp.bfloat16)
+    reduced_input = jnp.sum(lax.all_gather(partial_shrink, ("tp", "cores")), axis=0).astype(
+        jnp.bfloat16
+    )
     b_tiles = jnp.take(b_chosen, tile_seg, axis=0).reshape(tile_count, groups, rank_size, 2, narrow)
     gate_adapter_delta = jnp.einsum(
         "tkr,tmrw->tkmw",

time: 644 us -> 611 us (0.949)
  blocking collectives: 70 us -> 0 us
  waiting for transfers between devices: 71.2 us -> 105 us
    psum x1 -> x0, blocking collectives: 70 us -> none  [per_device(): lax.psum(partial_shrink, ('tp', 'cores')).astype(jnp.bfloat16)]
    all_to_all x1, waiting for transfers between devices: 28.9 us -> 69.2 us  [per_device(): lax.all_to_all(local_up_factor, ('tp', 'cores'), split_axis=1, concat_axi...]
    all_gather x1, waiting for transfers between devices: 37.6 us -> 0.01 us  [per_device(): gathered = lax.all_gather(tokens, ('tp', 'cores'), axis=1, tiled=True)]
    all_to_all x1, waiting for transfers between devices: 4.43 us -> 21.3 us  [per_device(): lax.all_to_all(local_down_factor, ('tp', 'cores'), split_axis=1, concat_a...]
    all_gather x0 -> x1, waiting for transfers between devices: none -> 13.9 us  [per_device(): lax.all_gather(partial_shrink, ('tp', 'cores'))]
    unnamed x23 -> x27, local copies, waits for them, and re-layouts: 101 us -> 101 us
    unnamed x3 -> x4, other arithmetic: 28.6 us -> 28.7 us
  transfers between devices with their start and end apart: 5 -> 6, of which waited for: 3 -> 3; matrix products, arithmetic and copies ran while one was open for 41% -> 56% of each run, Pallas kernels for 0% -> 0%
where the time goes in v1:
time: 611 us; the launch traced here: 601 us
  local copies, waits for them, and re-layouts  299 us (49%)
  waiting for transfers between devices  105 us (17%)
  matrix products  99.1 us (16%)
  other arithmetic  63.3 us (10%)
  starting transfers between devices  21.2 us (3%)
  between operations  13.8 us (2%)
    unnamed x27, local copies, waits for them, and re-layouts  101 us
    dot_general x1, local copies, waits for them, and re-layouts, per_device(): jnp.dot(gathered, gate_up_weight.reshape(full_width, 2 * local_hidden_wid...  83.7 us
    dot_general x1, matrix products, per_device(): jnp.dot(gathered, gate_up_weight.reshape(full_width, 2 * local_hidden_wid...  81 us
    all_to_all x1, waiting for transfers between devices, per_device(): lax.all_to_all(local_up_factor, ('tp', 'cores'), split_axis=1, concat_axi...  69.2 us
    unnamed x4, other arithmetic  28.7 us
    gather x4, local copies, waits for them, and re-layouts, per_device(): jnp.take(b_chosen, tile_seg, axis=0)  24.6 us
    all_to_all x1, waiting for transfers between devices, per_device(): lax.all_to_all(local_down_factor, ('tp', 'cores'), split_axis=1, concat_a...  21.3 us
    all_gather x1, waiting for transfers between devices, per_device(): lax.all_gather(partial_shrink, ('tp', 'cores'))  13.9 us
  transfers between devices with their start and end apart: 6, of which 3 were waited for; matrix products, arithmetic and copies ran while one was open for 56% of the time, Pallas kernels for 0%

profile of v1, /device:TPU:0, one launch (start us, length us, event | category | flops | bytes accessed | tf_op | source)
XLA Modules:
  0.0 601.0 jit_solution(11660585580552339724)
XLA Ops:
  11.1 7.3 %reduce.3 = bf16[8,65536]{1,0:T(8,128)(2,1)S(1)} reduce(bf16[8,1,65536]{2,1,0:T(2,128)(2,1)S(1)} %bitcast.110, bf16[]{:T(256)} %broadcast.154), dimensions={1}, to_apply=%bitcast.86.reduce_sub_computation | reduce | bytes 2097154
  20.2 7.3 %all-to-all-start = ((bf16[8,2,32768]{2,1,0:T(2,128)(2,1)}), bf16[8,2,32768]{2,1,0:T(2,128)(2,1)S(1)}, u32[]{:S(2)}, u32[]{:S(2)}) async-start(bf16[8,2,32768]{2,1,0:T(2,128)(2,1)} %reshape.207), calls=%async_computation | async-start | bytes 2097152 | tf_op jit(solution)/shard_map/all_to_all | solution.py:42
  33.4 13.0 %reduce.2 = bf16[8,131072]{1,0:T(8,128)(2,1)S(1)} reduce(bf16[8,1,131072]{2,1,0:T(2,128)(2,1)} %bitcast.103, bf16[]{:T(256)} %broadcast.154), dimensions={1}, to_apply=%bitcast.84.reduce_sub_computation | reduce | bytes 4194306
  49.5 21.3 %all-to-all-done = bf16[8,2,32768]{2,1,0:T(2,128)(2,1)S(1)} async-done(((bf16[8,2,32768]{2,1,0:T(2,128)(2,1)}), bf16[8,2,32768]{2,1,0:T(2,128)(2,1)S(1)}, u32[]{:S(2)}, u32[]{:S(2)}) %all-to-all-start) | async-done | bytes 1048608 | tf_op jit(solution)/shard_map/all_to_all | solution.py:42
  75.4 5.8 reshape.208
  95.0 69.2 %all-to-all-done.2 = bf16[8,2,65536]{2,1,0:T(2,128)(2,1)S(1)} async-done(((bf16[8,2,65536]{2,1,0:T(2,128)(2,1)}), bf16[8,2,65536]{2,1,0:T(2,128)(2,1)S(1)}, u32[]{:S(2)}, u32[]{:S(2)}) %all-to-all-start.2) | async-done | bytes 2097184 | tf_op jit(solution)/shard_map/all_to_all | solution.py:43
  164.2 4.7 all-to-all-start.1
  173.2 4.9 copy.79
  189.7 5.8 fusion.8
  195.4 5.0 all-to-all-start.3
  201.1 44.3 %copy.69 = bf16[1024,8,2,2048]{3,1,2,0:T(8,128)(2,1)} copy(bf16[1024,8,2,2048]{3,2,1,0:T(2,128)(2,1)} %bitcast.34) | data formatting | bytes 134217728
  245.4 83.7 %copy.48 = bf16[4096,8192]{1,0:T(8,128)(2,1)} copy(bf16[4096,8192]{0,1:T(8,128)(2,1)} %bitcast.1) | data formatting | bytes 134217728 | tf_op jit(solution)/shard_map/dot_general | solution.py:55
  332.3 5.4 gather_fusion.2
  337.6 7.9 %gather.27 = bf16[8,1024,256]{2,1,0:T(8,128)(2,1)} reshape(bf16[8,4,65536]{2,1,0:T(4,128)(2,1)} %gather_fusion.2) | data formatting | bytes 8388608 | tf_op jit(solution)/shard_map/jit(_take)/gather | solution.py:63
  345.5 5.2 copy.78
  351.8 5.4 gather_fusion.5
  357.2 5.5 gather_fusion.6
  362.7 10.3 %copy.70 = bf16[128,8,32,256]{3,2,1,0:T(8,128)(2,1)S(1)} copy(bf16[128,8,32,256]{3,1,2,0:T(8,128)(2,1)} %bitcast.105) | data formatting | bytes 33554432
  373.0 13.7 %dynamic-slice_reduce_fusion = bf16[1024,4,256]{2,1,0:T(4,128)(2,1)S(1)} fusion(bf16[1024,4,8,256]{3,2,1,0:T(8,128)(2,1)S(1)} %bitcast.101, s32[]{:T(128)S(6)} %select_n.80), kind=kLoop, calls=%fused_computation.27 | loop fusion | bytes 4194308 | tf_op jit(solution)/shard_map/dynamic_slice | solution.py:66
  389.4 4.8 fusion.9
  394.2 8.4 %pad_maximum_fusion = bf16[8,4,131072]{2,1,0:T(4,128)(2,1)} fusion(bf16[8,4,65536]{2,1,0:T(4,128)(2,1)} %gather_fusion.6, bf16[8,4,65536]{2,1,0:T(4,128)(2,1)} %gather_fusion.5), kind=kLoop, calls=%fused_computation.15 | loop fusion | flops 16777216 | bytes 16777216
  402.6 12.6 %reshape.202 = bf16[8,4,128,2,512]{4,3,2,1,0:T(2,128)(2,1)} reshape(bf16[8,4,131072]{2,1,0:T(4,128)(2,1)} %pad_maximum_fusion) | data formatting | bytes 16777216 | tf_op jit(solution)/shard_map/jit(_take)/gather | solution.py:76
  415.2 8.2 %copy_select_fusion = bf16[8,4,128,2,512]{4,2,1,0,3:T(8,128)(2,1)} fusion(bf16[8,4,128,2,512]{4,3,2,1,0:T(2,128)(2,1)} %reshape.202, pred[8]{0:T(512)(128)(4,1)S(1)} %compare_and_fusion.1), kind=kLoop, calls=%fused_computation.16 | loop fusion | flops 4194304 | bytes 16777224 | tf_op jit(solution)/shard_map/jit(_take)/select_n | solution.py:76
  423.4 81.0 %fusion = f32[1024,2,2048]{2,0,1:T(8,128)} fusion(bf16[2,2048,8192]{2,1,0:T(8,128)(2,1)} %bitcast.2, bf16[1024,8192]{1,0:T(8,128)(2,1)} %all-gather.4.cloned.1.call-done), kind=kOutput, calls=%fused_computation.7 | convolution fusion | flops 68719476736 | bytes 100663296 | tf_op jit(solution)/shard_map/dot_general | solution.py:55
  504.4 13.9 %all-gather.6.cloned.1.call-done = f32[64,128,256]{2,1,0:T(8,128)} async-done(((f32[8,128,256]{2,1,0:T(8,128)}), f32[64,128,256]{2,1,0:T(8,128)}) %all-gather.6.cloned.1.call-update) | async-done | bytes 8388624 | tf_op jit(solution)/shard_map/all_gather | solution.py:73
  522.4 6.7 %broadcast_multiply_fusion.1 = f32[8,128,4,512]{3,1,2,0:T(8,128)} fusion(bf16[8,4,128,2,512]{4,2,1,0,3:T(8,128)(2,1)} %copy_select_fusion, bf16[8,128,256]{2,1,0:T(8,128)(2,1)S(1)} %reduce_sum.22), kind=kOutput, calls=%fused_computation.24 | convolution fusion | flops 538968064 | bytes 12845056 | tf_op jit(solution)/shard_map/tkr,tmrw->tkmw/dot_general | solution.py:77
  529.0 6.7 %broadcast_multiply_fusion = f32[8,128,4,512]{3,1,2,0:T(8,128)} fusion(bf16[8,4,128,2,512]{4,2,1,0,3:T(8,128)(2,1)} %copy_select_fusion, bf16[8,128,256]{2,1,0:T(8,128)(2,1)S(1)} %reduce_sum.22), kind=kOutput, calls=%fused_computation.23 | convolution fusion | flops 538968064 | bytes 12845056 | tf_op jit(solution)/shard_map/tkr,tmrw->tkmw/dot_general | solution.py:83
  535.7 12.0 %copy.60 = f32[8,128,4,512]{3,2,1,0:T(4,128)} copy(f32[8,128,4,512]{3,1,2,0:T(8,128)} %broadcast_multiply_fusion) | data formatting | bytes 16777216 | tf_op jit(solution)/shard_map/mul | solution.py:92
  547.7 10.9 %copy.72 = f32[128,8,4,512]{3,1,2,0:T(8,128)} copy(f32[128,8,4,512]{3,2,1,0:T(4,128)} %bitcast.95) | data formatting | bytes 16777216
  558.6 12.0 %copy.59 = f32[8,128,4,512]{3,2,1,0:T(4,128)} copy(f32[8,128,4,512]{3,1,2,0:T(8,128)} %broadcast_multiply_fusion.1) | data formatting | bytes 16777216 | tf_op jit(solution)/shard_map/mul | solution.py:89
  570.6 11.0 %copy.71 = f32[128,8,4,512]{3,1,2,0:T(8,128)} copy(f32[128,8,4,512]{3,2,1,0:T(4,128)} %bitcast.96) | data formatting | bytes 16777216
  581.6 12.4 %fusion.4 = bf16[1024,2048]{1,0:T(8,128)(2,1)} fusion(f32[1024,2048]{1,0:T(8,128)S(1)} %bitcast.99, f32[1024,2,2048]{2,0,1:T(8,128)} %fusion, f32[1024,2048]{1,0:T(8,128)} %bitcast.100), kind=kLoop, calls=%fused_computation.12 | loop fusion | flops 16777216 | bytes 37748736 | tf_op jit(solution)/shard_map/convert_element_type | solution.py:95
  (57 shorter events, 61.3 us)
Async XLA Ops:
  6.5 21.8 %copy-start = (s32[8]{0:T(128)S(1)}, s32[8]{0:T(128)}, u32[]{:S(2)}) copy-start(s32[8]{0:T(128)} %param.13) | copy-start | bytes 100
  11.1 17.2 %copy-start.4 = (s32[4,3]{1,0:T(4,128)S(1)}, s32[4,3]{1,0:T(4,128)}, u32[]{:S(2)}) copy-start(s32[4,3]{1,0:T(4,128)} %param.11) | copy-start | bytes 148
  18.3 10.9 %copy-start.3 = (bf16[1,1,8,128,1024]{4,3,2,1,0:T(8,128)(2,1)S(1)}, bf16[1,1,8,128,1024]{4,3,2,1,0:T(8,128)(2,1)}, u32[]{:S(2)}) copy-start(bf16[1,1,8,128,1024]{4,3,2,1,0:T(8,128)(2,1)} %param.10) | copy-start | bytes 6291460
  20.2 50.6 %all-to-all-start = ((bf16[8,2,32768]{2,1,0:T(2,128)(2,1)}), bf16[8,2,32768]{2,1,0:T(2,128)(2,1)S(1)}, u32[]{:S(2)}, u32[]{:S(2)}) async-start(bf16[8,2,32768]{2,1,0:T(2,128)(2,1)} %reshape.207), calls=%async_computation | async-start | bytes 2097152 | tf_op jit(solution)/shard_map/all_to_all | solution.py:42
  27.5 335.2 %all-gather.4.cloned.1.call-start = ((), (), s32[]{:S(2)}) async-start(), calls=%async_computation.4 | async-start | bytes 18874368 | tf_op jit(solution)/shard_map/all_gather | solution.py:54
  70.8 1.0 copy-start.2
  71.8 92.4 %all-to-all-start.2 = ((bf16[8,2,65536]{2,1,0:T(2,128)(2,1)}), bf16[8,2,65536]{2,1,0:T(2,128)(2,1)S(1)}, u32[]{:S(2)}, u32[]{:S(2)}) async-start(bf16[8,2,65536]{2,1,0:T(2,128)(2,1)} %reshape.205), calls=%async_computation.2 | async-start | bytes 4194304 | tf_op jit(solution)/shard_map/all_to_all | solution.py:43
  164.2 31.2 %all-to-all-start.1 = ((bf16[4,3,1,65536]{3,1,2,0:T(4,128)(2,1)}), bf16[4,3,1,65536]{3,1,2,0:T(4,128)(2,1)}, u32[]{:S(2)}, u32[]{:S(2)}) async-start(bf16[4,3,1,65536]{3,1,2,0:T(4,128)(2,1)} %select_bitcast_fusion), calls=%async_computation.1 | async-start | bytes 4194304 | tf_op jit(solution)/shard_map/all_to_all | solution.py:49
  195.4 5.5 copy-start.5
  195.4 150.1 %all-to-all-start.3 = ((bf16[4,3,1,131072]{3,1,2,0:T(4,128)(2,1)}), bf16[4,3,1,131072]{3,1,2,0:T(4,128)(2,1)}, u32[]{:S(2)}, u32[]{:S(2)}) async-start(bf16[4,3,1,131072]{3,1,2,0:T(4,128)(2,1)} %fusion.8), calls=%async_computation.3 | async-start | bytes 8388608 | tf_op jit(solution)/shard_map/all_to_all | solution.py:50
  200.4 317.9 %all-gather.6.cloned.1.call-start = ((), (), s32[]{:S(2)}) async-start(), calls=%async_computation.5 | async-start | bytes 9437184 | tf_op jit(solution)/shard_map/all_gather | solution.py:73
  570.6 11.0 %slice-start = ((s8[8388608]{0:T(1024)(128)(4,1)}), s8[4194304]{0:T(1024)(128)(4,1)S(1)}, s32[]{:S(2)}) async-start(s8[8388608]{0:T(1024)(128)(4,1)} %bitcast.97), calls=%async_computation.6 | async-start | bytes 8388608
  570.6 11.0 %slice-start.1 = ((s8[8388608]{0:T(1024)(128)(4,1)}), s8[4194304]{0:T(1024)(128)(4,1)S(1)}, s32[]{:S(2)}) async-start(s8[8388608]{0:T(1024)(128)(4,1)} %bitcast.97), calls=%async_computation.7 | async-start | bytes 8388608
  581.6 12.4 %copy-start.1 = (s32[8]{0:T(128)S(1)}, s32[8]{0:T(128)}, u32[]{:S(2)}) copy-start(s32[8]{0:T(128)} %param.13) | copy-start | bytes 100
Sparse Core Ops, SparseCore 0:
  30.5 280.7 all-gather.3
  394.3 123.9 all-gather.5
